TPU v7x, 512 devices: a whole 4x8x8 slice. The times are simulated.
512 devices in a mesh: coil: 32 (over x, y), slab: 16 (over z, core).
Axes of the slice: x: 4, y: 8, z: 8, core: 2. Of those that a mesh axis runs over, the one named last changes fastest.
Arguments:
- adjoint_data: float32 [16, 192, 384], P('slab', 'coil'), may hold values from -80 to 80
- denoised: float32 [16, 192, 384], P('slab', 'coil'), may hold values from -8 to 8, as said below
- sensitivity: float32 [32, 16, 192, 384], P('coil', 'slab'), may hold values from -2 to 2, as said below
- kernel: float32 [16, 384, 384], P(None, 'slab'), may hold values from 0.1 to 2, as said below
- conv_in: bfloat16 [54, 64], replicated, may hold values from -0.875 to 0.875
- conv_mid: bfloat16 [1728, 64], replicated, may hold values from -0.15625 to 0.15625
- conv_out: bfloat16 [1728, 2], replicated, may hold values from -0.15625 to 0.15625
Outputs:
- solution: float32 [16, 192, 384], P('slab', 'coil')
- refined: float32 [16, 192, 384], P('slab', 'coil')
Inputs may be any that keep to these rules, and one draw needn't show every extreme that they name: `denoised`: real and imaginary parts of the previous cascade's image. `sensitivity`: real and imaginary parts of the coil maps. Positive kernel values.
All inputs are finite; a program needn't handle non-finite values.
Results may differ from a plain program's by a relative error of at most 0.0023.
Values may be sent and summed in bfloat16 or wider, within the bound.
A program may use at most 64 MiB of HBM per device.

v0:
```python
import math
import jax
import jax.numpy as jnp
from jax import lax
from jax.sharding import PartitionSpec as P

ITERS = 2
reg_weight = 0.5
highest = lax.Precision.HIGHEST


def with_halo(cells, sides, width):
    for axis, dim in sides:
        count = lax.axis_size(axis)
        ends = count - 1
        head = lax.slice_in_dim(cells, 0, width, axis=dim)
        tail = lax.slice_in_dim(cells, cells.shape[dim] - width, cells.shape[dim], axis=dim)
        cells = jnp.concatenate(
            [
                lax.ppermute(tail, axis, [(i, (i + 1) % count) for i in range(ends)]),
                cells,
                lax.ppermute(head, axis, [((i + 1) % count, i) for i in range(ends)]),
            ],
            axis=dim,
        )
    return cells


def dft_tables(out_len, in_len, length, inverse):
    out_index = lax.broadcasted_iota(jnp.int32, (out_len, in_len), 0)
    in_index = lax.broadcasted_iota(jnp.int32, (out_len, in_len), 1)
    phases = (out_index * in_index % length).astype(jnp.float32) * (2.0 * math.pi / length)
    if inverse:
        return (jnp.cos(phases) / length, jnp.sin(phases) / length)
    return (jnp.cos(phases), -jnp.sin(phases))


def block_matrix(tables):
    cos_table = tables[0]
    sin_table = tables[1]
    upper = jnp.concatenate([cos_table.T, sin_table.T], axis=1)
    lower = jnp.concatenate([-sin_table.T, cos_table.T], axis=1)
    return jnp.concatenate([upper, lower], axis=0)


def along_axis(values, tables, einsum_form):
    half_len = values.shape[-1] // 2
    real_part = jnp.einsum(einsum_form, tables[0], values, precision=highest)
    imag_part = jnp.einsum(einsum_form, tables[1], values, precision=highest)
    return jnp.concatenate(
        [
            real_part[..., :half_len] - imag_part[..., half_len:],
            real_part[..., half_len:] + imag_part[..., :half_len],
        ],
        axis=-1,
    )


def complex_product(factor_one, factor_two):
    half_len = factor_one.shape[-1] // 2
    real_one = factor_one[..., :half_len]
    imag_one = factor_one[..., half_len:]
    real_two = factor_two[..., :half_len]
    imag_two = factor_two[..., half_len:]
    return jnp.concatenate(
        [real_one * real_two - imag_one * imag_two, real_one * imag_two + imag_one * real_two],
        axis=-1,
    )


def conj_product(factor_one, factor_two):
    half_len = factor_one.shape[-1] // 2
    real_one = factor_one[..., :half_len]
    imag_one = factor_one[..., half_len:]
    real_two = factor_two[..., :half_len]
    imag_two = factor_two[..., half_len:]
    return jnp.concatenate(
        [real_one * real_two + imag_one * imag_two, real_one * imag_two - imag_one * real_two],
        axis=-1,
    )


def convolve(features, weights, in_channels):
    padded = with_halo(features, (("coil", 1), ("slab", 0)), 1)
    depth_here = features.shape[0]
    rows_here = features.shape[1]
    side_len = features.shape[2] // in_channels
    padded_cube = padded.reshape(depth_here + 2, rows_here + 2, side_len, in_channels)
    padded_cube = jnp.pad(padded_cube, ((0, 0), (0, 0), (1, 1), (0, 0)))
    width_taps = 9 * in_channels
    running = None
    for shift_z in range(3):
        tap_list = [
            padded_cube[
                shift_z : shift_z + depth_here,
                shift_x : shift_x + rows_here,
                shift_y : shift_y + side_len,
                :,
            ]
            for shift_x in range(3)
            for shift_y in range(3)
        ]
        patches = jnp.concatenate(tap_list, axis=-1).reshape(-1, width_taps)
        partial_sum = jnp.dot(
            patches,
            weights[shift_z * width_taps : (shift_z + 1) * width_taps],
            preferred_element_type=jnp.float32,
        )
        running = partial_sum if shift_z == 0 else running + partial_sum
    return running


def shards(adjoint_data, denoised, sensitivity, kernel, conv_in, conv_mid, conv_out):
    side_len = sensitivity.shape[2]
    depth_len = kernel.shape[0]
    grid_len = kernel.shape[2]
    fwd_plane = dft_tables(grid_len, side_len, grid_len, False)
    inv_plane = dft_tables(side_len, grid_len, grid_len, True)
    fwd_depth = dft_tables(depth_len, depth_len, depth_len, False)
    inv_depth = dft_tables(depth_len, depth_len, depth_len, True)
    fwd_last = block_matrix(fwd_plane)
    inv_last = block_matrix(inv_plane)

    def total_squares(residual):
        return lax.psum(jnp.sum(residual * residual), ("coil", "slab"))

    right_side = adjoint_data + reg_weight * denoised
    solution = jnp.zeros_like(right_side)
    residual = right_side
    direction = right_side
    norm_now = total_squares(residual)
    for iteration in range(ITERS):
        products = complex_product(
            sensitivity, lax.all_gather(direction, "coil", axis=1, tiled=True)[None]
        )
        products = jnp.matmul(products, fwd_last, precision=highest)
        spread = along_axis(products, fwd_plane, "kn,cznw->czkw")
        apply_pencil = lax.all_to_all(spread, "slab", split_axis=2, concat_axis=1, tiled=True)
        spectrum = along_axis(apply_pencil, fwd_depth, "kn,cnxw->ckxw")
        shape_now = spectrum.shape
        split_form = spectrum.reshape(shape_now[0], shape_now[1], shape_now[2], 2, grid_len)
        weighted = split_form * kernel[None, :, :, None, :]
        returned = along_axis(weighted.reshape(shape_now), inv_depth, "kn,cnxw->ckxw")
        slab_back = lax.all_to_all(returned, "slab", split_axis=1, concat_axis=2, tiled=True)
        image_back = along_axis(slab_back, inv_plane, "kn,cznw->czkw")
        image_back = jnp.matmul(image_back, inv_last, precision=highest)
        coil_sum = jnp.sum(conj_product(sensitivity, image_back), axis=0)
        summed = lax.psum_scatter(coil_sum, "coil", scatter_dimension=1, tiled=True)
        image_out = summed + reg_weight * direction
        local_curv = jnp.sum(direction * image_out)
        image_out, local_curv = (image_out, local_curv)
        curvature = lax.psum(local_curv, ("coil", "slab"))
        step_size = norm_now / curvature
        solution = solution + step_size * direction
        if iteration + 1 < ITERS:
            residual = residual - step_size * image_out
            norm_next = total_squares(residual)
            direction = residual + norm_next / norm_now * direction
            norm_now = norm_next
    depth_here = solution.shape[0]
    rows_here = solution.shape[1]
    channels = jnp.stack([solution[..., :side_len], solution[..., side_len:]], axis=-1).astype(
        jnp.bfloat16
    )
    first_map = convolve(channels.reshape(depth_here, rows_here, 2 * side_len), conv_in, 2)
    hidden_count = conv_mid.shape[1]
    hidden_one = (
        jax.nn.relu(first_map)
        .astype(jnp.bfloat16)
        .reshape(depth_here, rows_here, side_len * hidden_count)
    )
    second_map = convolve(hidden_one, conv_mid, hidden_count)
    hidden_two = (
        jax.nn.relu(second_map)
        .astype(jnp.bfloat16)
        .reshape(depth_here, rows_here, side_len * hidden_count)
    )
    third_map = convolve(hidden_two, conv_out, hidden_count).reshape(
        depth_here, rows_here, side_len, 2
    )
    refined = solution + jnp.concatenate([third_map[..., 0], third_map[..., 1]], axis=-1)
    return (solution, refined)


def solution(mesh):
    placed = (
        P("slab", "coil", None),
        P("slab", "coil", None),
        P("coil", "slab", None, None),
        P(None, "slab", None),
        P(),
        P(),
        P(),
    )
    return jax.shard_map(
        shards,
        mesh=mesh,
        in_specs=placed,
        out_specs=(P("slab", "coil", None), P("slab", "coil", None)),
        check_vma=False,
    )
```

profile of v0, /device:TPU:249, one launch (start us, length us, event | category | flops | bytes accessed | tf_op | source)
XLA Modules:
  0.0 1028.2 jit_solution(9897725327793448658)
XLA Ops:
  10.4 37.1 %all_gather.6 = f32[1,192,384]{2,0,1:T(1,128)S(1)} all-gather(f32[1,6,384]{2,0,1:T(1,128)S(1)} %copy.111), channel_id=1, replica_groups=mesh['coil'=32,'slab'=16] {'coil'}, dimensions={1}, use_global_device_ids=true | all-gather | bytes 304128 | tf_op jit(solution)/shard_map/all_gather | solution.py:134
  48.9 4.0 convolution_bitcast_fusion.10
  52.9 4.0 convolution_bitcast_fusion.11
  57.1 2.7 copy.112
  59.8 21.2 %all-to-all-start = ((f32[1,1,384,768]{3,1,0,2:T(1,128)}), f32[1,1,384,768]{3,1,0,2:T(1,128)S(1)}, u32[]{:S(2)}, u32[]{:S(2)}) async-start(f32[1,1,384,768]{3,1,0,2:T(1,128)} %copy.112), calls=%async_computation | async-start | bytes 2359296 | tf_op jit(solution)/shard_map/all_to_all | solution.py:138
  81.2 1.7 mul.249
  82.9 2.2 mul.250
  85.1 25.0 %all-to-all-done = f32[1,1,384,768]{3,1,0,2:T(1,128)S(1)} async-done(((f32[1,1,384,768]{3,1,0,2:T(1,128)}), f32[1,1,384,768]{3,1,0,2:T(1,128)S(1)}, u32[]{:S(2)}, u32[]{:S(2)}) %all-to-all-start) | async-done | bytes 1179680 | tf_op jit(solution)/shard_map/all_to_all | solution.py:138
  115.9 1.7 copy.116
  117.6 5.2 all-to-all-start.1
  123.0 1.5 fusion.59
  124.5 2.4 fusion.25
  127.0 24.9 %all-to-all-done.1 = f32[1,16,24,768]{3,2,0,1:T(8,128)S(1)} async-done(((f32[1,16,24,768]{3,2,0,1:T(8,128)}), f32[1,16,24,768]{3,2,0,1:T(8,128)S(1)}, u32[]{:S(2)}, u32[]{:S(2)}) %all-to-all-start.1) | async-done | bytes 1179680 | tf_op jit(solution)/shard_map/all_to_all | solution.py:144
  151.8 2.3 convolution_bitcast_fusion.14
  154.1 2.3 convolution_bitcast_fusion.15
  162.2 145.9 %all-reduce.9.cloned.1.call-done = f32[1,192,384]{2,0,1:T(1,128)} async-done(((f32[1,192,384]{2,0,1:T(1,128)}), f32[1,192,384]{2,0,1:T(1,128)}) %all-reduce.9.cloned.1.call-update) | async-done | bytes 294928
  309.4 99.0 %all-reduce.5 = (f32[]{:T(128)}, f32[]{:T(128)}) all-reduce(f32[]{:T(128)} %get-tuple-element.13, f32[]{:T(128)} %get-tuple-element.12), channel_id=1, replica_groups=mesh['coil'=32,'slab'=16] {'coil','slab'}, use_global_device_ids=true, to_apply=%region_1.2 | all-reduce | flops 2 | bytes 16 | tf_op jit(solution)/shard_map/psum | solution.py:125
  410.4 94.7 %psum.30 = f32[]{:T(128)} all-reduce(f32[]{:T(128)} %multiply_reduce_fusion), channel_id=1, replica_groups=mesh['coil'=32,'slab'=16] {'coil','slab'}, use_global_device_ids=true, to_apply=%region_6.7 | all-reduce | flops 1 | bytes 8 | tf_op jit(solution)/shard_map/psum | solution.py:125
  506.5 37.2 %all_gather.7 = f32[1,192,384]{2,0,1:T(1,128)S(1)} all-gather(f32[1,6,384]{2,0,1:T(1,128)S(1)} %copy.119), channel_id=1, replica_groups=mesh['coil'=32,'slab'=16] {'coil'}, dimensions={1}, use_global_device_ids=true | all-gather | bytes 304128 | tf_op jit(solution)/shard_map/all_gather | solution.py:134
  545.1 4.0 convolution_bitcast_fusion.8
  549.1 4.0 convolution_bitcast_fusion.9
  553.3 2.7 copy.120
  556.0 47.3 %all_to_all.16 = f32[1,1,384,768]{3,1,0,2:T(1,128)S(1)} all-to-all(f32[1,1,384,768]{3,1,0,2:T(1,128)} %copy.120), channel_id=1, replica_groups=mesh['coil'=32,'slab'=16] {'slab'}, dimensions={2} | all-to-all | bytes 2359296 | tf_op jit(solution)/shard_map/all_to_all | solution.py:138
  604.9 1.4 convolution_bitcast_fusion.3
  609.9 34.2 %all_to_all.17 = f32[1,16,24,768]{3,2,0,1:T(8,128)S(1)} all-to-all(f32[1,16,24,768]{3,2,0,1:T(8,128)S(1)} %copy.123), channel_id=1, replica_groups=mesh['coil'=32,'slab'=16] {'slab'}, dimensions={1} | all-to-all | bytes 2359296 | tf_op jit(solution)/shard_map/all_to_all | solution.py:144
  644.1 2.3 convolution_bitcast_fusion.12
  646.4 2.3 convolution_bitcast_fusion.13
  652.4 148.8 %all-reduce.11.cloned.1.call-done = f32[1,192,384]{2,0,1:T(1,128)} async-done(((f32[1,192,384]{2,0,1:T(1,128)}), f32[1,192,384]{2,0,1:T(1,128)}) %all-reduce.11.cloned.1.call-update) | async-done | bytes 294928
  802.5 98.9 %psum.31 = f32[]{:T(128)} all-reduce(f32[]{:T(128)} %fusion.74), channel_id=1, replica_groups=mesh['coil'=32,'slab'=16] {'coil','slab'}, use_global_device_ids=true, to_apply=%region_9.10 | all-reduce | flops 1 | bytes 8 | tf_op jit(solution)/shard_map/psum | solution.py:152
  903.1 5.1 collective-permute-start
  908.2 1.9 collective-permute-start.1
  910.3 5.3 collective-permute-done.1
  915.8 4.0 collective-permute-start.3
  919.8 3.5 collective-permute-start.2
  924.0 1.5 fusion.193
  925.5 1.6 fusion.192
  927.2 4.2 concatenate.143
  932.1 1.7 concatenate.142
  934.6 1.7 concatenate.141
  938.3 1.9 collective-permute-start.4
  940.3 3.4 collective-permute-start.5
  943.7 3.6 collective-permute-done.5
  947.4 4.0 collective-permute-start.7
  951.4 4.7 collective-permute-start.6
  961.2 1.7 pad_slice_fusion.18
  962.9 2.0 pad_slice_fusion.19
  964.8 3.1 concatenate.146
  967.9 2.2 fusion.71
  970.1 2.7 concatenate.147
  972.8 2.4 convolution_add_fusion.1
  975.2 2.9 concatenate.148
  978.1 1.5 fusion.3
  980.2 1.9 collective-permute-start.8
  982.1 3.4 collective-permute-start.9
  985.5 4.0 collective-permute-done.9
  989.6 2.7 collective-permute-start.11
  992.3 5.5 collective-permute-start.10
  1003.2 1.7 pad_slice_fusion
  1004.9 2.0 pad_slice_fusion.1
  1006.8 3.1 concatenate.151
  1009.9 1.8 fusion.115
  1011.7 2.7 concatenate.152
  1014.4 1.8 convolution_add_fusion.5
  1016.2 2.9 concatenate.153
  (128 shorter events, 47.5 us)
Async XLA Ops:
  7.2 40.4 %copy-start = (f32[1,1,192,384]{3,2,1,0:T(8,128)S(1)}, f32[1,1,192,384]{3,2,1,0:T(8,128)}, u32[]{:S(2)}) copy-start(f32[1,1,192,384]{3,2,1,0:T(8,128)} %param.9) | copy-start | bytes 884740
  8.3 39.4 %copy-start.5 = (f32[192,384]{1,0:T(8,128)}, f32[192,384]{1,0:T(8,128)S(1)}, u32[]{:S(2)}) copy-start(f32[192,384]{1,0:T(8,128)S(1)} %fusion.66) | copy-start | bytes 884740
  9.5 39.4 %copy-start.7 = (f32[192,384]{1,0:T(8,128)}, f32[192,384]{1,0:T(8,128)S(1)}, u32[]{:S(2)}) copy-start(f32[192,384]{1,0:T(8,128)S(1)} %get-tuple-element.133) | copy-start | bytes 884740
  9.5 39.4 %copy-start.9 = (f32[192,384]{1,0:T(8,128)}, f32[192,384]{1,0:T(8,128)S(1)}, u32[]{:S(2)}) copy-start(f32[192,384]{1,0:T(8,128)S(1)} %get-tuple-element.134) | copy-start | bytes 884740
  59.8 21.2 %copy-start.2 = (f32[16,24,384]{2,1,0:T(8,128)S(1)}, f32[16,24,384]{2,1,0:T(8,128)}, u32[]{:S(2)}) copy-start(f32[16,24,384]{2,1,0:T(8,128)} %param.10) | copy-start | bytes 1769476
  59.8 50.2 %all-to-all-start = ((f32[1,1,384,768]{3,1,0,2:T(1,128)}), f32[1,1,384,768]{3,1,0,2:T(1,128)S(1)}, u32[]{:S(2)}, u32[]{:S(2)}) async-start(f32[1,1,384,768]{3,1,0,2:T(1,128)} %copy.112), calls=%async_computation | async-start | bytes 2359296 | tf_op jit(solution)/shard_map/all_to_all | solution.py:138
  117.6 34.2 %all-to-all-start.1 = ((f32[1,16,24,768]{3,2,0,1:T(8,128)}), f32[1,16,24,768]{3,2,0,1:T(8,128)S(1)}, u32[]{:S(2)}, u32[]{:S(2)}) async-start(f32[1,16,24,768]{3,2,0,1:T(8,128)} %copy.116), calls=%async_computation.1 | async-start | bytes 2359296 | tf_op jit(solution)/shard_map/all_to_all | solution.py:144
  122.8 185.3 %all-reduce.9.cloned.1.call-start = ((), (), s32[]{:S(2)}) async-start(), calls=%async_computation.4 | async-start | bytes 589824
  156.5 1.0 copy-start.3
  160.1 383.8 %copy-start.6 = (f32[192,384]{1,0:T(8,128)S(1)}, f32[192,384]{1,0:T(8,128)}, u32[]{:S(2)}) copy-start(f32[192,384]{1,0:T(8,128)} %copy-done.5) | copy-start | bytes 884740
  160.1 383.8 %copy-start.8 = (f32[192,384]{1,0:T(8,128)S(1)}, f32[192,384]{1,0:T(8,128)}, u32[]{:S(2)}) copy-start(f32[192,384]{1,0:T(8,128)} %copy-done.7) | copy-start | bytes 884740
  160.2 383.8 %copy-start.10 = (f32[192,384]{1,0:T(8,128)S(1)}, f32[192,384]{1,0:T(8,128)}, u32[]{:S(2)}) copy-start(f32[192,384]{1,0:T(8,128)} %copy-done.9) | copy-start | bytes 884740
  160.2 641.0 %all-reduce.11.cloned.1.call-start = ((), (), s32[]{:S(2)}) async-start(), calls=%async_computation.5 | async-start | bytes 589824
  648.8 1.0 copy-start.4
  903.1 7.1 collective-permute-start
  908.2 7.5 collective-permute-start.1
  915.8 7.5 collective-permute-start.3
  919.8 4.0 collective-permute-start.2
  936.2 0.8 copy-start.12
  938.3 5.3 collective-permute-start.4
  940.3 6.9 collective-permute-start.5
  947.4 9.9 collective-permute-start.7
  951.4 7.1 collective-permute-start.6
  975.2 2.9 copy-start.1
  980.2 5.3 collective-permute-start.8
  982.1 7.4 collective-permute-start.9
  989.6 9.7 collective-permute-start.11
  992.3 8.1 collective-permute-start.10
  1016.2 2.9 copy-start.11
Sparse Core Ops, SparseCore 0:
  160.3 147.8 all-reduce.8
  652.5 148.5 all-reduce.10
where the time goes:
time: 1030 us
  blocking collectives  449 us (44%)
  waiting for transfers between devices  362 us (35%)
  starting transfers between devices  68.6 us (7%)
  local copies, waits for them, and re-layouts  64.6 us (6%)
  matrix products  52.4 us (5%)
  between operations  19.8 us (2%)
  other arithmetic  12 us (1%)
    unnamed x4, waiting for transfers between devices  295 us
    psum x2, blocking collectives, total_squares(): return lax.psum(jnp.sum(residual * residual), ('coil', 'slab'))  194 us
    psum x1, blocking collectives, shards(): curvature = lax.psum(local_curv, ('coil', 'slab'))  98.9 us
    all_gather x2, blocking collectives, shards(): lax.all_gather(direction, 'coil', axis=1, tiled=True)[None]  74.3 us
    all_to_all x1, blocking collectives, shards(): lax.all_to_all(spread, 'slab', split_axis=2, concat_axis=1, tiled=True)  47.3 us
    all_to_all x1, blocking collectives, shards(): lax.all_to_all(returned, 'slab', split_axis=1, concat_axis=2, tiled=True)  34.2 us
    concatenate x12, local copies, waits for them, and re-layouts, convolve(): patches = jnp.concatenate(tap_list, axis=-1).reshape(-1, width_taps)  26.8 us
    all_to_all x1, waiting for transfers between devices, shards(): lax.all_to_all(spread, 'slab', split_axis=2, concat_axis=1, tiled=True)  25 us
  transfers between devices with their start and end apart: 16, of which 12 were waited for; matrix products, arithmetic and copies ran while one was open for 1% of the time, Pallas kernels for 0%

commit v1 on v0

--- a/solution.py
+++ b/solution.py
@@ -131,7 +131,10 @@
     norm_now = total_squares(residual)
     for iteration in range(ITERS):
         products = complex_product(
-            sensitivity, lax.all_gather(direction, "coil", axis=1, tiled=True)[None]
+            sensitivity,
+            jnp.concatenate(
+                lax.all_to_all(jnp.stack([direction] * lax.axis_size("coil")), "coil", 0, 0), axis=1
+            )[None],
         )
         products = jnp.matmul(products, fwd_last, precision=highest)
         spread = along_axis(products, fwd_plane, "kn,cznw->czkw")

time: 1030 us -> 978 us (0.950)
  blocking collectives: 449 us -> 382 us
    all_gather x2 -> x0, blocking collectives: 74.3 us -> none  [shards(): lax.all_gather(direction, 'coil', axis=1, tiled=True)[None]]
    all_to_all x0 -> x1, blocking collectives: none -> 18.3 us  [shards(): lax.all_to_all(jnp.stack([direction] * lax.axis_size('coil')), 'coil', 0, 0)]
    all_to_all x1, starting transfers between devices: 21.2 us -> 10.4 us  [shards(): lax.all_to_all(spread, 'slab', split_axis=2, concat_axis=1, tiled=True)]
    all_to_all x1, blocking collectives: 47.3 us -> 36.9 us  [shards(): lax.all_to_all(spread, 'slab', split_axis=2, concat_axis=1, tiled=True)]
  transfers between devices with their start and end apart: 16 -> 17, of which waited for: 12 -> 13; matrix products, arithmetic and copies ran while one was open for 1% -> 1% of each run, Pallas kernels for 0% -> 0%
where the time goes in v1:
time: 978 us; the launch traced here: 967 us
  blocking collectives  382 us (39%)
  waiting for transfers between devices  367 us (38%)
  starting transfers between devices  66.6 us (7%)
  local copies, waits for them, and re-layouts  66.4 us (7%)
  matrix products  52.6 us (5%)
  between operations  20.1 us (2%)
  other arithmetic  12 us (1%)
    unnamed x4, waiting for transfers between devices  293 us
    psum x2, blocking collectives, total_squares(): return lax.psum(jnp.sum(residual * residual), ('coil', 'slab'))  194 us
    psum x1, blocking collectives, shards(): curvature = lax.psum(local_curv, ('coil', 'slab'))  98.9 us
    all_to_all x1, blocking collectives, shards(): lax.all_to_all(spread, 'slab', split_axis=2, concat_axis=1, tiled=True)  36.9 us
    all_to_all x1, blocking collectives, shards(): lax.all_to_all(returned, 'slab', split_axis=1, concat_axis=2, tiled=True)  34.2 us
    concatenate x12, local copies, waits for them, and re-layouts, convolve(): patches = jnp.concatenate(tap_list, axis=-1).reshape(-1, width_taps)  26.7 us
    all_to_all x1, waiting for transfers between devices, shards(): lax.all_to_all(spread, 'slab', split_axis=2, concat_axis=1, tiled=True)  25 us
    all_to_all x1, waiting for transfers between devices, shards(): lax.all_to_all(returned, 'slab', split_axis=1, concat_axis=2, tiled=True)  24.8 us
  transfers between devices with their start and end apart: 17, of which 13 were waited for; matrix products, arithmetic and copies ran while one was open for 1% of the time, Pallas kernels for 0%

profile of v1, /device:TPU:249, one launch (start us, length us, event | category | flops | bytes accessed | tf_op | source)
XLA Modules:
  0.0 967.0 jit_solution(10580463897557781071)
XLA Ops:
  8.8 9.1 all-to-all-start
  20.2 6.6 all-to-all-done
  28.6 4.0 convolution_bitcast_fusion.10
  32.6 4.1 convolution_bitcast_fusion.11
  37.0 2.7 copy.123
  39.7 10.4 %all-to-all-start.1 = ((f32[1,1,384,768]{3,1,0,2:T(1,128)}), f32[1,1,384,768]{3,1,0,2:T(1,128)S(1)}, u32[]{:S(2)}, u32[]{:S(2)}) async-start(f32[1,1,384,768]{3,1,0,2:T(1,128)} %copy.123), calls=%async_computation.1 | async-start | bytes 2359296 | tf_op jit(solution)/shard_map/all_to_all | solution.py:141
  50.2 1.7 mul.249
  51.9 2.2 mul.250
  54.1 25.0 %all-to-all-done.1 = f32[1,1,384,768]{3,1,0,2:T(1,128)S(1)} async-done(((f32[1,1,384,768]{3,1,0,2:T(1,128)}), f32[1,1,384,768]{3,1,0,2:T(1,128)S(1)}, u32[]{:S(2)}, u32[]{:S(2)}) %all-to-all-start.1) | async-done | bytes 1179680 | tf_op jit(solution)/shard_map/all_to_all | solution.py:141
  85.0 1.7 copy.127
  86.7 5.2 all-to-all-start.2
  92.0 1.5 fusion.59
  93.5 2.6 fusion.25
  96.1 24.8 %all-to-all-done.2 = f32[1,16,24,768]{3,2,0,1:T(8,128)S(1)} async-done(((f32[1,16,24,768]{3,2,0,1:T(8,128)}), f32[1,16,24,768]{3,2,0,1:T(8,128)S(1)}, u32[]{:S(2)}, u32[]{:S(2)}) %all-to-all-start.2) | async-done | bytes 1179680 | tf_op jit(solution)/shard_map/all_to_all | solution.py:147
  120.9 2.3 convolution_bitcast_fusion.14
  123.3 2.3 convolution_bitcast_fusion.15
  131.2 145.5 %all-reduce.9.cloned.1.call-done = f32[1,192,384]{2,0,1:T(1,128)} async-done(((f32[1,192,384]{2,0,1:T(1,128)}), f32[1,192,384]{2,0,1:T(1,128)}) %all-reduce.9.cloned.1.call-update) | async-done | bytes 294928
  278.0 99.0 %all-reduce.5 = (f32[]{:T(128)}, f32[]{:T(128)}) all-reduce(f32[]{:T(128)} %get-tuple-element.13, f32[]{:T(128)} %get-tuple-element.12), channel_id=1, replica_groups=mesh['coil'=32,'slab'=16] {'coil','slab'}, use_global_device_ids=true, to_apply=%region_1.2 | all-reduce | flops 2 | bytes 16 | tf_op jit(solution)/shard_map/psum | solution.py:125
  379.0 94.7 %psum.30 = f32[]{:T(128)} all-reduce(f32[]{:T(128)} %multiply_reduce_fusion), channel_id=1, replica_groups=mesh['coil'=32,'slab'=16] {'coil','slab'}, use_global_device_ids=true, to_apply=%region_6.7 | all-reduce | flops 1 | bytes 8 | tf_op jit(solution)/shard_map/psum | solution.py:125
  475.3 18.3 %all_to_all.46 = f32[32,1,6,384]{3,1,2,0:T(1,128)S(1)} all-to-all(f32[32,1,6,384]{3,1,2,0:T(1,128)S(1)} %stack.11), channel_id=1, replica_groups=mesh['coil'=32,'slab'=16] {'coil'}, dimensions={0} | all-to-all | bytes 589824 | tf_op jit(solution)/shard_map/all_to_all | solution.py:136
  495.4 4.0 convolution_bitcast_fusion.8
  499.4 4.0 convolution_bitcast_fusion.9
  503.6 2.7 copy.132
  506.3 36.9 %all_to_all.47 = f32[1,1,384,768]{3,1,0,2:T(1,128)S(1)} all-to-all(f32[1,1,384,768]{3,1,0,2:T(1,128)} %copy.132), channel_id=1, replica_groups=mesh['coil'=32,'slab'=16] {'slab'}, dimensions={2} | all-to-all | bytes 2359296 | tf_op jit(solution)/shard_map/all_to_all | solution.py:141
  549.8 34.2 %all_to_all.48 = f32[1,16,24,768]{3,2,0,1:T(8,128)S(1)} all-to-all(f32[1,16,24,768]{3,2,0,1:T(8,128)S(1)} %copy.135), channel_id=1, replica_groups=mesh['coil'=32,'slab'=16] {'slab'}, dimensions={1} | all-to-all | bytes 2359296 | tf_op jit(solution)/shard_map/all_to_all | solution.py:147
  584.0 2.3 convolution_bitcast_fusion.12
  586.3 2.3 convolution_bitcast_fusion.13
  592.3 147.3 %all-reduce.11.cloned.1.call-done = f32[1,192,384]{2,0,1:T(1,128)} async-done(((f32[1,192,384]{2,0,1:T(1,128)}), f32[1,192,384]{2,0,1:T(1,128)}) %all-reduce.11.cloned.1.call-update) | async-done | bytes 294928
  741.0 98.9 %psum.31 = f32[]{:T(128)} all-reduce(f32[]{:T(128)} %fusion.74), channel_id=1, replica_groups=mesh['coil'=32,'slab'=16] {'coil','slab'}, use_global_device_ids=true, to_apply=%region_9.10 | all-reduce | flops 1 | bytes 8 | tf_op jit(solution)/shard_map/psum | solution.py:155
  841.6 5.1 collective-permute-start
  846.7 1.9 collective-permute-start.1
  848.8 5.3 collective-permute-done.1
  854.3 4.0 collective-permute-start.3
  858.3 3.2 collective-permute-start.2
  862.5 1.5 fusion.194
  864.0 1.6 fusion.193
  865.6 4.4 concatenate.143
  870.9 1.7 concatenate.142
  873.3 1.7 concatenate.141
  877.1 1.9 collective-permute-start.4
  879.0 3.4 collective-permute-start.5
  882.4 3.6 collective-permute-done.5
  886.1 4.0 collective-permute-start.7
  890.1 4.5 collective-permute-start.6
  899.9 1.7 pad_slice_fusion.18
  901.6 2.0 pad_slice_fusion.19
  903.5 3.1 concatenate.146
  906.6 2.2 fusion.71
  908.8 2.7 concatenate.147
  911.5 2.4 convolution_add_fusion.1
  913.9 2.7 concatenate.148
  916.7 1.5 fusion.3
  918.8 1.9 collective-permute-start.8
  920.7 3.4 collective-permute-start.9
  924.1 4.0 collective-permute-done.9
  928.2 2.7 collective-permute-start.11
  930.9 5.8 collective-permute-start.10
  941.7 1.7 pad_slice_fusion
  943.4 2.0 pad_slice_fusion.1
  945.4 3.1 concatenate.151
  948.5 1.8 fusion.115
  950.3 2.7 concatenate.152
  953.0 1.9 convolution_add_fusion.5
  955.0 2.7 concatenate.153
  (141 shorter events, 50.6 us)
Async XLA Ops:
  8.7 18.6 %copy-start = (f32[1,1,192,384]{3,2,1,0:T(8,128)S(1)}, f32[1,1,192,384]{3,2,1,0:T(8,128)}, u32[]{:S(2)}) copy-start(f32[1,1,192,384]{3,2,1,0:T(8,128)} %param.9) | copy-start | bytes 884740
  8.8 18.0 %all-to-all-start = ((f32[32,1,6,384]{3,1,2,0:T(1,128)}), f32[32,1,6,384]{3,1,2,0:T(1,128)S(1)}, u32[]{:S(2)}, u32[]{:S(2)}) async-start(f32[32,1,6,384]{3,1,2,0:T(1,128)} %stack.10), calls=%async_computation | async-start | bytes 589824 | tf_op jit(solution)/shard_map/all_to_all | solution.py:136
  19.0 8.5 copy-start.11
  20.2 8.5 copy-start.13
  20.2 8.5 copy-start.15
  39.7 10.4 %copy-start.8 = (f32[16,24,384]{2,1,0:T(8,128)S(1)}, f32[16,24,384]{2,1,0:T(8,128)}, u32[]{:S(2)}) copy-start(f32[16,24,384]{2,1,0:T(8,128)} %param.10) | copy-start | bytes 1769476
  39.7 39.4 %all-to-all-start.1 = ((f32[1,1,384,768]{3,1,0,2:T(1,128)}), f32[1,1,384,768]{3,1,0,2:T(1,128)S(1)}, u32[]{:S(2)}, u32[]{:S(2)}) async-start(f32[1,1,384,768]{3,1,0,2:T(1,128)} %copy.123), calls=%async_computation.1 | async-start | bytes 2359296 | tf_op jit(solution)/shard_map/all_to_all | solution.py:141
  86.7 34.2 %all-to-all-start.2 = ((f32[1,16,24,768]{3,2,0,1:T(8,128)}), f32[1,16,24,768]{3,2,0,1:T(8,128)S(1)}, u32[]{:S(2)}, u32[]{:S(2)}) async-start(f32[1,16,24,768]{3,2,0,1:T(8,128)} %copy.127), calls=%async_computation.2 | async-start | bytes 2359296 | tf_op jit(solution)/shard_map/all_to_all | solution.py:147
  91.9 184.8 %all-reduce.9.cloned.1.call-start = ((), (), s32[]{:S(2)}) async-start(), calls=%async_computation.6 | async-start | bytes 589824
  125.6 1.0 copy-start.9
  129.3 610.4 %all-reduce.11.cloned.1.call-start = ((), (), s32[]{:S(2)}) async-start(), calls=%async_computation.7 | async-start | bytes 589824
  475.2 19.0 %copy-start.12 = (f32[192,384]{1,0:T(8,128)S(1)}, f32[192,384]{1,0:T(8,128)}, u32[]{:S(2)}) copy-start(f32[192,384]{1,0:T(8,128)} %copy-done.11) | copy-start | bytes 884740
  475.2 19.0 %copy-start.14 = (f32[192,384]{1,0:T(8,128)S(1)}, f32[192,384]{1,0:T(8,128)}, u32[]{:S(2)}) copy-start(f32[192,384]{1,0:T(8,128)} %copy-done.13) | copy-start | bytes 884740
  475.3 19.0 %copy-start.16 = (f32[192,384]{1,0:T(8,128)S(1)}, f32[192,384]{1,0:T(8,128)}, u32[]{:S(2)}) copy-start(f32[192,384]{1,0:T(8,128)} %copy-done.15) | copy-start | bytes 884740
  588.6 1.0 copy-start.10
  841.6 7.1 collective-permute-start
  846.7 7.5 collective-permute-start.1
  854.3 7.3 collective-permute-start.3
  858.3 4.0 collective-permute-start.2
  875.0 0.8 copy-start.18
  877.1 5.3 collective-permute-start.4
  879.0 6.9 collective-permute-start.5
  886.1 9.9 %collective-permute-start.7 = (bf16[1,8,12288]{2,1,0:T(8,128)(2,1)S(1)}, bf16[1,8,12288]{2,1,0:T(8,128)(2,1)S(1)}, u32[]{:S(2)}, u32[]{:S(2)}) collective-permute-start(bf16[1,8,12288]{2,1,0:T(8,128)(2,1)S(1)} %pad_maximum_fusion.6), channel_id=1, source_target_pairs={{1,0},{2,1},{3,2},{4,3},{5,4},{6,5},{7,6},{8,7},{9,8},{10,9},{11,1... | collective-permute-start | bytes 589832 | tf_op jit(solution)/shard_map/ppermute | solution.py:22
  890.1 7.1 collective-permute-start.6
  911.5 2.5 copy-start.1
  911.5 2.4 copy-start.2
  911.5 2.4 copy-start.3
  913.9 2.8 copy-start.7
  918.8 5.3 collective-permute-start.8
  920.7 7.4 collective-permute-start.9
  928.2 9.7 %collective-permute-start.11 = (bf16[1,8,12288]{2,1,0:T(8,128)(2,1)S(1)}, bf16[1,8,12288]{2,1,0:T(8,128)(2,1)S(1)}, u32[]{:S(2)}, u32[]{:S(2)}) collective-permute-start(bf16[1,8,12288]{2,1,0:T(8,128)(2,1)S(1)} %pad_maximum_fusion.7), channel_id=1, source_target_pairs={{1,0},{2,1},{3,2},{4,3},{5,4},{6,5},{7,6},{8,7},{9,8},{10,9},{11,1... | collective-permute-start | bytes 589832 | tf_op jit(solution)/shard_map/ppermute | solution.py:22
  930.9 8.1 collective-permute-start.10
  953.0 1.9 copy-start.4
  953.0 1.9 copy-start.5
  953.0 1.9 copy-start.6
  954.9 2.7 copy-start.17
Sparse Core Ops, SparseCore 0:
  129.4 147.2 all-reduce.8
  592.4 147.1 all-reduce.10
